TPU v7x, 32 devices: a whole 2x2x4 slice. The times are simulated.
32 devices in a mesh: pipe: 16 (over z, y, core), ctx: 2 (over x).
Axes of the slice: x: 2, y: 2, z: 4, core: 2. Of those that a mesh axis runs over, the one named last changes fastest.
Arguments:
- query_fwd: bfloat16 [16, 256, 4096], P('pipe', 'ctx'), may hold values from -110 to 110
- key_fwd: bfloat16 [16, 256, 1024], P('pipe', 'ctx'), may hold values from -4.5 to 4.5
- value_fwd: bfloat16 [16, 256, 1024], P('pipe', 'ctx'), may hold values from -6 to 6
- query_bwd: bfloat16 [16, 256, 4096], P('pipe', 'ctx'), may hold values from -110 to 110
- key_bwd: bfloat16 [16, 256, 1024], P('pipe', 'ctx'), may hold values from -4.5 to 4.5
- value_bwd: bfloat16 [16, 256, 1024], P('pipe', 'ctx'), may hold values from -6 to 6
- cotangent: bfloat16 [16, 256, 4096], P('pipe', 'ctx'), may hold values from -6 to 6
- documents: int32 [16, 2, 256], P('pipe'), may hold values from 0 to 3, never falling along the last dimension, each value on 1 to 128 neighbouring positions
Outputs:
- attended: bfloat16 [16, 256, 4096], P('pipe', 'ctx')
- query_grad: bfloat16 [16, 256, 4096], P('pipe', 'ctx')
- key_grad: bfloat16 [16, 256, 1024], P('pipe', 'ctx')
- value_grad: bfloat16 [16, 256, 1024], P('pipe', 'ctx')
Inputs may be any that keep to these rules, and one draw needn't show every extreme that they name: Along the last dimension ids never fall; 4 documents per slab, each of 1 to 128 positions, one of exactly 128.
All inputs are finite; a program needn't handle non-finite values.
Results may differ from a plain program's by a relative error of at most 0.0085.
Values may be sent and summed in bfloat16 or wider, within the bound.
A program may use at most 128 MiB of HBM per device.

v0:
```python
import jax
import jax.numpy as jnp
from jax import lax
from jax.sharding import PartitionSpec as P

KVH = 8
QBLK = 128


def passed_along(value, axis, steps):
    count = lax.axis_size(axis)
    pairs = [(source, (source + steps) % count) for source in range(count)]
    return lax.ppermute(value, axis, pairs)


def allowed_mask(query_places, query_documents, key_places, key_documents):
    causal = key_places[None, :] <= query_places[:, None]
    same_document = key_documents[None, :] == query_documents[:, None]
    return causal & same_document


def head_probs(query_head, key_head, allowed, score_scale):
    raw_scores = (
        jnp.einsum("rgd,kd->grk", query_head, key_head, preferred_element_type=jnp.float32)
        * score_scale
    )
    masked = jnp.where(allowed[None], raw_scores, jnp.float32(-1e30))
    row_max = jnp.max(masked, axis=-1, keepdims=True)
    exponent = jnp.exp(masked - row_max)
    return exponent / jnp.sum(exponent, axis=-1, keepdims=True)


def forward_all(
    queries, keys_all, values_all, query_places, query_documents, key_places, key_documents
):
    row_count, head_count, query_width = queries.shape
    head_size = keys_all.shape[2]
    score_scale = head_size ** (-0.5)
    block_count = row_count // QBLK
    query_blocks = queries.reshape(block_count, QBLK, head_count, query_width)
    place_blocks = query_places.reshape(block_count, QBLK)
    document_blocks = query_documents.reshape(block_count, QBLK)

    def forward_one_block(packed):
        query_block, place_block, document_block = packed
        allowed = allowed_mask(place_block, document_block, key_places, key_documents)

        def forward_one_head(head):
            query_head = lax.dynamic_index_in_dim(query_block, head, 1, False).reshape(
                QBLK, -1, head_size
            )
            key_head = lax.dynamic_index_in_dim(keys_all, head, 1, False)
            value_head = lax.dynamic_index_in_dim(values_all, head, 1, False)
            weights = head_probs(query_head, key_head, allowed, score_scale).astype(jnp.bfloat16)
            mixture = jnp.einsum(
                "grk,kd->rgd", weights, value_head, preferred_element_type=jnp.float32
            )
            return mixture.reshape(QBLK, query_width).astype(jnp.bfloat16)

        return jnp.moveaxis(
            lax.map(forward_one_head, jnp.arange(head_count, dtype=jnp.int32)), 0, 1
        )

    outcome = lax.map(forward_one_block, (query_blocks, place_blocks, document_blocks))
    return outcome.reshape(row_count, head_count, query_width)


def backward_all(
    queries, keys_all, values_all, cotan, query_places, query_documents, key_places, key_documents
):
    row_count, head_count, query_width = queries.shape
    head_size = keys_all.shape[2]
    score_scale = head_size ** (-0.5)
    block_count = row_count // QBLK
    query_blocks = queries.reshape(block_count, QBLK, head_count, query_width)
    cotan_blocks = cotan.reshape(block_count, QBLK, head_count, query_width)
    place_blocks = query_places.reshape(block_count, QBLK)
    document_blocks = query_documents.reshape(block_count, QBLK)

    def backward_one_block(totals, packed):
        query_block, cotan_block, place_block, document_block = packed
        allowed = allowed_mask(place_block, document_block, key_places, key_documents)

        def backward_one_head(head):
            query_head = lax.dynamic_index_in_dim(query_block, head, 1, False).reshape(
                QBLK, -1, head_size
            )
            cotan_head = lax.dynamic_index_in_dim(cotan_block, head, 1, False).reshape(
                QBLK, -1, head_size
            )
            key_head = lax.dynamic_index_in_dim(keys_all, head, 1, False)
            value_head = lax.dynamic_index_in_dim(values_all, head, 1, False)
            probability = head_probs(query_head, key_head, allowed, score_scale)
            weights = probability.astype(jnp.bfloat16)
            prob_grad = jnp.einsum(
                "rgd,kd->grk", cotan_head, value_head, preferred_element_type=jnp.float32
            )
            row_delta = jnp.sum(probability * prob_grad, axis=-1, keepdims=True)
            score_grad = (probability * (prob_grad - row_delta) * score_scale).astype(jnp.bfloat16)
            query_part = jnp.einsum(
                "grk,kd->rgd", score_grad, key_head, preferred_element_type=jnp.float32
            )
            key_part = jnp.einsum(
                "grk,rgd->kd", score_grad, query_head, preferred_element_type=jnp.float32
            )
            value_part = jnp.einsum(
                "grk,rgd->kd", weights, cotan_head, preferred_element_type=jnp.float32
            )
            return (
                query_part.reshape(QBLK, query_width).astype(jnp.bfloat16),
                key_part,
                value_part,
            )

        query_part, key_part, value_part = lax.map(
            backward_one_head, jnp.arange(head_count, dtype=jnp.int32)
        )
        new_totals = (
            totals[0] + jnp.moveaxis(key_part, 0, 1),
            totals[1] + jnp.moveaxis(value_part, 0, 1),
        )
        return (new_totals, jnp.moveaxis(query_part, 0, 1))

    empty_sum = jnp.zeros(keys_all.shape, jnp.float32)
    sums, query_grads = lax.scan(
        backward_one_block,
        (empty_sum, empty_sum),
        (query_blocks, cotan_blocks, place_blocks, document_blocks),
    )
    return (query_grads.reshape(row_count, head_count, query_width), sums[0], sums[1])


def on_device(query_fwd, key_fwd, value_fwd, query_bwd, key_bwd, value_bwd, cotangent, documents):
    shard_rows = query_fwd.shape[1]
    context_count = lax.axis_size("ctx")
    forward_docs = documents[0, 0]
    backward_docs = documents[0, 1]
    arrived = passed_along((query_fwd[0], key_fwd[0], value_fwd[0]), "pipe", 1)
    cotan_local = passed_along(cotangent[0], "pipe", -1)
    start = lax.axis_index("ctx") * shard_rows
    query_places = start + jnp.arange(shard_rows, dtype=jnp.int32)
    seq_length = shard_rows * context_count
    key_places = jnp.arange(seq_length, dtype=jnp.int32)
    keys_all, values_all = (
        lax.all_gather(arrived[1], "ctx", axis=0, tiled=True),
        lax.all_gather(arrived[2], "ctx", axis=0, tiled=True),
    )
    own_docs = lax.dynamic_slice_in_dim(forward_docs, start, shard_rows)
    outcome = forward_all(
        arrived[0].reshape(shard_rows, KVH, -1),
        keys_all.reshape(seq_length, KVH, -1),
        values_all.reshape(seq_length, KVH, -1),
        query_places,
        own_docs,
        key_places,
        forward_docs,
    )
    attended = outcome.reshape(1, shard_rows, -1)
    back_keys, back_values = (
        lax.all_gather(key_bwd[0], "ctx", axis=0, tiled=True),
        lax.all_gather(value_bwd[0], "ctx", axis=0, tiled=True),
    )
    back_own_docs = lax.dynamic_slice_in_dim(backward_docs, start, shard_rows)
    query_part, key_part, value_part = backward_all(
        query_bwd[0].reshape(shard_rows, KVH, -1),
        back_keys.reshape(seq_length, KVH, -1),
        back_values.reshape(seq_length, KVH, -1),
        cotan_local.reshape(shard_rows, KVH, -1),
        query_places,
        back_own_docs,
        key_places,
        backward_docs,
    )
    stacked = jnp.stack(
        (key_part.reshape(seq_length, -1), value_part.reshape(seq_length, -1)), axis=1
    )
    summed = lax.psum_scatter(stacked, "ctx", scatter_dimension=0, tiled=True)
    grads = (
        query_part.reshape(shard_rows, -1),
        summed[:, 0].astype(jnp.bfloat16),
        summed[:, 1].astype(jnp.bfloat16),
    )
    handed = passed_along((grads[0], grads[1], grads[2]), "pipe", -1)
    return (attended, handed[0][None], handed[1][None], handed[2][None])


def solution(mesh):
    in_specs = (
        P("pipe", "ctx", None),
        P("pipe", "ctx", None),
        P("pipe", "ctx", None),
        P("pipe", "ctx", None),
        P("pipe", "ctx", None),
        P("pipe", "ctx", None),
        P("pipe", "ctx", None),
        P("pipe", None, None),
    )
    out_specs = (
        P("pipe", "ctx", None),
        P("pipe", "ctx", None),
        P("pipe", "ctx", None),
        P("pipe", "ctx", None),
    )
    return jax.shard_map(
        on_device, mesh=mesh, in_specs=in_specs, out_specs=out_specs, check_vma=False
    )
```

profile of v0, /device:TPU:0, one launch (start us, length us, event | category | flops | bytes accessed | tf_op | source)
XLA Modules:
  0.0 230.4 jit_solution(735514472314002335)
XLA Ops:
  7.2 5.5 %collective-permute-start.3 = (bf16[128,4096]{1,0:T(8,128)(2,1)}, bf16[128,4096]{1,0:T(8,128)(2,1)}, u32[]{:S(2)}, u32[]{:S(2)}) collective-permute-start(bf16[128,4096]{1,0:T(8,128)(2,1)} %bitcast.204), channel_id=1, source_target_pairs={{0,30},{2,0},{4,2},{6,4},{8,6},{10,8},{12,10},{14,12},{16,14},{18,... | collective-permute-start | bytes 3145736 | tf_op jit(solution)/shard_map/ppermute | solution.py:13
  12.8 1.6 copy.34
  14.8 8.7 %all-gather = bf16[1,256,1024]{1,2,0:T(8,128)(2,1)} all-gather(bf16[1,128,1024]{1,2,0:T(8,128)(2,1)S(1)} %copy.33), channel_id=2, replica_groups=mesh['pipe'=16,'ctx'=2] {'ctx'}, dimensions={1}, use_global_device_ids=true | all-gather | bytes 786432 | tf_op jit(solution)/shard_map/all_gather | solution.py:160
  23.5 7.2 %all-gather.1 = bf16[1,256,1024]{1,2,0:T(8,128)(2,1)} all-gather(bf16[1,128,1024]{1,2,0:T(8,128)(2,1)S(1)} %copy.35), channel_id=3, replica_groups=mesh['pipe'=16,'ctx'=2] {'ctx'}, dimensions={1}, use_global_device_ids=true | all-gather | bytes 786432 | tf_op jit(solution)/shard_map/all_gather | solution.py:161
  30.7 1.6 copy.36
  32.4 93.4 %while.45 = (s32[]{:T(128)}, bf16[8,128,512]{1,2,0:T(8,128)(2,1)S(1)}, f32[8,256,128]{2,1,0:T(8,128)}, f32[8,256,128]{2,1,0:T(8,128)}, s32[8]{0:T(128)S(1)}, /*i...) while((s32[]{:T(128)}, ...), condition=%wide.region_8.9_spmd.clone, body=%wide.region_4.8_spmd.clone.sunk | while | flops 204507648 | bytes 15842571 | solution.py:115
  35.2 2.0 fusion.131
  38.3 2.2 fusion.132
  40.4 1.5 convolution_convert_fusion.5
  42.0 2.1 fusion.133
  46.9 2.0 fusion.131
  50.0 2.2 fusion.132
  52.1 1.5 convolution_convert_fusion.5
  53.7 2.1 fusion.133
  58.6 2.0 fusion.131
  61.6 2.2 fusion.132
  63.8 1.5 convolution_convert_fusion.5
  65.4 2.1 fusion.133
  70.2 2.0 fusion.131
  73.3 2.2 fusion.132
  75.5 1.5 convolution_convert_fusion.5
  77.0 2.1 fusion.133
  81.9 2.0 fusion.131
  83.9 1.1 convolution_bitcast_fusion.4
  85.0 2.2 fusion.132
  87.1 1.5 convolution_convert_fusion.5
  88.7 2.1 fusion.133
  93.6 2.0 fusion.131
  95.6 1.1 convolution_bitcast_fusion.4
  96.6 2.2 fusion.132
  98.8 1.5 convolution_convert_fusion.5
  100.4 2.1 fusion.133
  105.2 2.0 fusion.131
  107.2 1.1 convolution_bitcast_fusion.4
  108.3 2.2 fusion.132
  110.5 1.5 convolution_convert_fusion.5
  112.0 2.1 fusion.133
  116.9 2.0 fusion.131
  120.0 2.2 fusion.132
  122.1 1.5 convolution_convert_fusion.5
  123.7 2.1 fusion.133
  125.8 1.8 copy.40
  127.8 1.8 copy.41
  129.7 1.1 stack_reshape.7
  130.8 2.8 %pad_maximum_fusion = f32[256,2,1024]{2,0,1:T(8,128)} fusion(f32[256,1,1024]{2,0,1:T(8,128)} %stack_reshape.7, f32[256,1,1024]{2,0,1:T(8,128)S(1)} %stack_reshape.6), kind=kLoop, calls=%fused_computation.70 | loop fusion | flops 524288 | bytes 4194304 | tf_op jit(solution)/shard_map/stack | solution.py:174
  134.9 18.7 %collective-permute-done = bf16[128,1024]{1,0:T(8,128)(2,1)S(1)} collective-permute-done((bf16[128,1024]{1,0:T(8,128)(2,1)S(1)}, bf16[128,1024]{1,0:T(8,128)(2,1)S(1)}, u32[]{:S(2)}, u32[]{:S(2)}) %collective-permute-start) | collective-permute-done | bytes 262176 | tf_op jit(solution)/shard_map/ppermute | solution.py:13
  153.6 14.0 %all_gather.12 = bf16[256,1024]{1,0:T(8,128)(2,1)S(1)} all-gather(bf16[128,1024]{1,0:T(8,128)(2,1)S(1)} %collective-permute-done), channel_id=1, replica_groups=mesh['pipe'=16,'ctx'=2] {'ctx'}, dimensions={0}, use_global_device_ids=true | all-gather | bytes 786432 | tf_op jit(solution)/shard_map/all_gather | solution.py:146
  168.6 7.1 %all_gather.13 = bf16[256,1024]{0,1:T(8,128)(2,1)S(1)} all-gather(bf16[128,1024]{0,1:T(8,128)(2,1)S(1)} %collective-permute-done.1), channel_id=1, replica_groups=mesh['pipe'=16,'ctx'=2] {'ctx'}, dimensions={0}, use_global_device_ids=true | all-gather | bytes 786432 | tf_op jit(solution)/shard_map/all_gather | solution.py:145
  175.6 1.3 copy.51
  176.9 2.5 %collective-permute-start.4 = (bf16[128,4096]{1,0:T(8,128)(2,1)}, bf16[128,4096]{1,0:T(8,128)(2,1)}, u32[]{:S(2)}, u32[]{:S(2)}) collective-permute-start(bf16[128,4096]{1,0:T(8,128)(2,1)} %copy.51), channel_id=1, source_target_pairs={{0,30},{2,0},{4,2},{6,4},{8,6},{10,8},{12,10},{14,12},{16,14},{18,... | collective-permute-start | bytes 3145736 | tf_op jit(solution)/shard_map/ppermute | solution.py:13
  180.1 1.3 convert.4
  183.5 33.1 %while.44 = (s32[]{:T(128)}, bf16[8,128,512]{1,2,0:T(8,128)(2,1)S(1)}, s32[8]{0:T(128)S(1)}, bf16[256,8,128]{0,2,1:T(8,128)(2,1)}, bf16[256,8,128]{0,2,1:T(8,128...) while((s32[]{:T(128)}, ...), condition=%wide.region_3.4_spmd.clone, body=%wide.region_0.3_spmd.clone.sunk | while | flops 102007808 | bytes 2791607 | solution.py:61
  186.5 1.1 convolution_convert_fusion.4
  190.6 1.1 convolution_convert_fusion.4
  194.8 1.1 convolution_convert_fusion.4
  198.9 1.1 convolution_convert_fusion.4
  203.0 1.1 convolution_convert_fusion.4
  207.2 1.1 convolution_convert_fusion.4
  211.3 1.1 convolution_convert_fusion.4
  215.4 1.1 convolution_convert_fusion.4
  216.6 1.3 copy.50
  217.9 2.3 copy.81
  220.2 1.7 copy.82
  221.9 1.7 copy.83
  (158 shorter events, 28.3 us)
Async XLA Ops:
  7.2 7.2 %copy-start.2 = (bf16[1,128,1024]{2,1,0:T(8,128)(2,1)S(1)}, bf16[1,128,1024]{2,1,0:T(8,128)(2,1)}, u32[]{:S(2)}) copy-start(bf16[1,128,1024]{2,1,0:T(8,128)(2,1)} %param.16) | copy-start | bytes 786436
  7.2 7.4 %copy-start.3 = (bf16[1,128,1024]{2,1,0:T(8,128)(2,1)S(1)}, bf16[1,128,1024]{2,1,0:T(8,128)(2,1)}, u32[]{:S(2)}) copy-start(bf16[1,128,1024]{2,1,0:T(8,128)(2,1)} %param.17) | copy-start | bytes 786436
  7.2 7.6 %copy-start.5 = (s32[1,2,256]{2,1,0:T(2,128)S(1)}, s32[1,2,256]{2,1,0:T(2,128)}, u32[]{:S(2)}) copy-start(s32[1,2,256]{2,1,0:T(2,128)} %param.19) | copy-start | bytes 6148
  7.2 172.9 %reduce-scatter.2.cloned.1.call-start = ((), (), s32[]{:S(2)}) async-start(), calls=%async_computation.1 | async-start | bytes 3145728 | tf_op jit(solution)/shard_map/reduce_scatter | solution.py:177
  7.2 23.4 %collective-permute-start.3 = (bf16[128,4096]{1,0:T(8,128)(2,1)}, bf16[128,4096]{1,0:T(8,128)(2,1)}, u32[]{:S(2)}, u32[]{:S(2)}) collective-permute-start(bf16[128,4096]{1,0:T(8,128)(2,1)} %bitcast.204), channel_id=1, source_target_pairs={{0,30},{2,0},{4,2},{6,4},{8,6},{10,8},{12,10},{14,12},{16,14},{18,... | collective-permute-start | bytes 3145736 | tf_op jit(solution)/shard_map/ppermute | solution.py:13
  32.4 4.7 %copy-start = (bf16[128,8,512]{0,2,1:T(8,128)(2,1)}, bf16[128,8,512]{0,2,1:T(8,128)(2,1)S(1)}, u32[]{:S(2)}) copy-start(bf16[128,8,512]{0,2,1:T(8,128)(2,1)S(1)} %get-tuple-element.495) | copy-start | bytes 3145732 | tf_op jit(solution)/shard_map/while/body/eval_jaxpr/while
  42.0 2.1 copy-start.1
  44.1 4.7 %copy-start = (bf16[128,8,512]{0,2,1:T(8,128)(2,1)}, bf16[128,8,512]{0,2,1:T(8,128)(2,1)S(1)}, u32[]{:S(2)}) copy-start(bf16[128,8,512]{0,2,1:T(8,128)(2,1)S(1)} %get-tuple-element.495) | copy-start | bytes 3145732 | tf_op jit(solution)/shard_map/while/body/eval_jaxpr/while
  53.7 2.1 copy-start.1
  55.8 4.7 %copy-start = (bf16[128,8,512]{0,2,1:T(8,128)(2,1)}, bf16[128,8,512]{0,2,1:T(8,128)(2,1)S(1)}, u32[]{:S(2)}) copy-start(bf16[128,8,512]{0,2,1:T(8,128)(2,1)S(1)} %get-tuple-element.495) | copy-start | bytes 3145732 | tf_op jit(solution)/shard_map/while/body/eval_jaxpr/while
  65.3 2.1 copy-start.1
  67.5 4.7 %copy-start = (bf16[128,8,512]{0,2,1:T(8,128)(2,1)}, bf16[128,8,512]{0,2,1:T(8,128)(2,1)S(1)}, u32[]{:S(2)}) copy-start(bf16[128,8,512]{0,2,1:T(8,128)(2,1)S(1)} %get-tuple-element.495) | copy-start | bytes 3145732 | tf_op jit(solution)/shard_map/while/body/eval_jaxpr/while
  77.0 2.1 copy-start.1
  79.1 4.7 %copy-start = (bf16[128,8,512]{0,2,1:T(8,128)(2,1)}, bf16[128,8,512]{0,2,1:T(8,128)(2,1)S(1)}, u32[]{:S(2)}) copy-start(bf16[128,8,512]{0,2,1:T(8,128)(2,1)S(1)} %get-tuple-element.495) | copy-start | bytes 3145732 | tf_op jit(solution)/shard_map/while/body/eval_jaxpr/while
  88.7 2.1 copy-start.1
  90.8 4.7 %copy-start = (bf16[128,8,512]{0,2,1:T(8,128)(2,1)}, bf16[128,8,512]{0,2,1:T(8,128)(2,1)S(1)}, u32[]{:S(2)}) copy-start(bf16[128,8,512]{0,2,1:T(8,128)(2,1)S(1)} %get-tuple-element.495) | copy-start | bytes 3145732 | tf_op jit(solution)/shard_map/while/body/eval_jaxpr/while
  100.4 2.1 copy-start.1
  102.5 4.7 %copy-start = (bf16[128,8,512]{0,2,1:T(8,128)(2,1)}, bf16[128,8,512]{0,2,1:T(8,128)(2,1)S(1)}, u32[]{:S(2)}) copy-start(bf16[128,8,512]{0,2,1:T(8,128)(2,1)S(1)} %get-tuple-element.495) | copy-start | bytes 3145732 | tf_op jit(solution)/shard_map/while/body/eval_jaxpr/while
  112.0 2.1 copy-start.1
  114.2 4.7 %copy-start = (bf16[128,8,512]{0,2,1:T(8,128)(2,1)}, bf16[128,8,512]{0,2,1:T(8,128)(2,1)S(1)}, u32[]{:S(2)}) copy-start(bf16[128,8,512]{0,2,1:T(8,128)(2,1)S(1)} %get-tuple-element.495) | copy-start | bytes 3145732 | tf_op jit(solution)/shard_map/while/body/eval_jaxpr/while
  123.7 2.1 copy-start.1
  133.6 0.9 copy-start.6
  133.6 1.0 copy-start.4
  133.6 45.9 %collective-permute-start.2 = (bf16[128,4096]{1,0:T(8,128)(2,1)}, bf16[128,4096]{1,0:T(8,128)(2,1)S(1)}, u32[]{:S(2)}, u32[]{:S(2)}) collective-permute-start(bf16[128,4096]{1,0:T(8,128)(2,1)} %bitcast.205), channel_id=1, source_target_pairs={{0,2},{2,4},{4,6},{6,8},{8,10},{10,12},{12,14},{14,16},{16,18},{18... | collective-permute-start | bytes 3145736 | tf_op jit(solution)/shard_map/ppermute | solution.py:13
  134.5 19.1 %collective-permute-start = (bf16[128,1024]{1,0:T(8,128)(2,1)S(1)}, bf16[128,1024]{1,0:T(8,128)(2,1)S(1)}, u32[]{:S(2)}, u32[]{:S(2)}) collective-permute-start(bf16[128,1024]{1,0:T(8,128)(2,1)S(1)} %bitcast.206), channel_id=1, source_target_pairs={{0,2},{2,4},{4,6},{6,8},{8,10},{10,12},{12,14},{14,16},{16,18},{18... | collective-permute-start | bytes 786440 | tf_op jit(solution)/shard_map/ppermute | solution.py:13
  134.8 33.8 %collective-permute-start.1 = (bf16[128,1024]{0,1:T(8,128)(2,1)S(1)}, bf16[128,1024]{0,1:T(8,128)(2,1)S(1)}, u32[]{:S(2)}, u32[]{:S(2)}) collective-permute-start(bf16[128,1024]{0,1:T(8,128)(2,1)S(1)} %bitcast.201), channel_id=1, source_target_pairs={{0,2},{2,4},{4,6},{6,8},{8,10},{10,12},{12,14},{14,16},{16,18},{18... | collective-permute-start | bytes 786440 | tf_op jit(solution)/shard_map/ppermute | solution.py:13
  176.9 41.0 %collective-permute-start.4 = (bf16[128,4096]{1,0:T(8,128)(2,1)}, bf16[128,4096]{1,0:T(8,128)(2,1)}, u32[]{:S(2)}, u32[]{:S(2)}) collective-permute-start(bf16[128,4096]{1,0:T(8,128)(2,1)} %copy.51), channel_id=1, source_target_pairs={{0,30},{2,0},{4,2},{6,4},{8,6},{10,8},{12,10},{14,12},{16,14},{18,... | collective-permute-start | bytes 3145736 | tf_op jit(solution)/shard_map/ppermute | solution.py:13
  182.3 35.7 %collective-permute-start.5 = (bf16[128,1024]{1,0:T(8,128)(2,1)}, bf16[128,1024]{1,0:T(8,128)(2,1)}, u32[]{:S(2)}, u32[]{:S(2)}) collective-permute-start(bf16[128,1024]{1,0:T(8,128)(2,1)} %get-tuple-element.282), channel_id=1, source_target_pairs={{0,30},{2,0},{4,2},{6,4},{8,6},{10,8},{12,10},{14,12},{16,14},{18,... | collective-permute-start | bytes 786440 | tf_op jit(solution)/shard_map/ppermute | solution.py:13
  183.3 34.6 %collective-permute-start.6 = (bf16[128,1024]{1,0:T(8,128)(2,1)}, bf16[128,1024]{1,0:T(8,128)(2,1)}, u32[]{:S(2)}, u32[]{:S(2)}) collective-permute-start(bf16[128,1024]{1,0:T(8,128)(2,1)} %get-tuple-element.281), channel_id=1, source_target_pairs={{0,30},{2,0},{4,2},{6,4},{8,6},{10,8},{12,10},{14,12},{16,14},{18,... | collective-permute-start | bytes 786440 | tf_op jit(solution)/shard_map/ppermute | solution.py:13
Sparse Core Ops, SparseCore 0:
  133.7 38.8 reduce-scatter.1
where the time goes:
time: 233 us; the launch traced here: 230 us
  matrix products  84.8 us (36%)
  blocking collectives  36.9 us (16%)
  local copies, waits for them, and re-layouts  31.2 us (13%)
  loops' own time  29.5 us (13%)
  waiting for transfers between devices  18.8 us (8%)
  between operations  14.2 us (6%)
  starting transfers between devices  9.32 us (4%)
  other arithmetic  5.69 us (2%)
    sub x16, matrix products, head_probs(): exponent = jnp.exp(masked - row_max)  18.8 us
    ppermute x7, waiting for transfers between devices, passed_along(): return lax.ppermute(value, axis, pairs)  18.8 us
    dot_general x8, matrix products, backward_one_head(): jnp.einsum('grk,rgd->kd', score_grad, query_head, preferred_element_type=...  17.3 us
    dot_general x8, matrix products, backward_one_head(): jnp.einsum('grk,rgd->kd', weights, cotan_head, preferred_element_type=jnp...  16.9 us
    another operation x1, loops' own time, backward_one_block(): lax.map(backward_one_head, jnp.arange(head_count, dtype=jnp.int32))  16 us
    all_gather x1, blocking collectives, on_device(): lax.all_gather(arrived[2], 'ctx', axis=0, tiled=True)  14 us
    another operation x1, loops' own time, forward_one_block(): lax.map(forward_one_head, jnp.arange(head_count, dtype=jnp.int32))  13.5 us
    dot_general x8, matrix products, backward_one_head(): jnp.einsum('grk,kd->rgd', score_grad, key_head, preferred_element_type=jn...  12.2 us
  transfers between devices with their start and end apart: 8, of which 1 were waited for; matrix products, arithmetic and copies ran while one was open for 12% of the time, Pallas kernels for 0%

commit v1 on v0

v1 whole, which is shorter than its diff:
```python
import functools
import math

import jax
import jax.numpy as jnp
from jax import lax
from jax.experimental import pallas as pl
from jax.experimental.pallas import tpu as pltpu
from jax.sharding import PartitionSpec as P

KVH = 8
F32 = jnp.float32
BF16 = jnp.bfloat16


def matmul(a, b, da, db):
    return lax.dot_general(a, b, (((da,), (db,)), ((), ())), preferred_element_type=F32)


def kernel(
    sections, shards, qf, kf, vf, qb, kb, vb, cot, docs, att_o, dq_o, dk_o, dv_o,
    qf_v, qb_v, g_v, kv, att_s, dq_s, dkv_s, dkv, part, docs_v, docs_r, bias,
    local_sem, docs_sem, kv_send, kv_recv, g_send, g_recv, part_send, part_recv,
    wide_send, wide_recv, dkv_send, dkv_recv,
):
    rows, width = qf.shape[1], qf.shape[2]
    narrow = kf.shape[2]
    hd = narrow // KVH
    group = width // narrow
    qw = group * hd
    scale = hd ** (-0.5)
    section, me = lax.axis_index("pipe"), lax.axis_index("ctx")
    after = lax.rem(section + 1, sections)
    before = lax.rem(section + sections - 1, sections)
    even = lax.rem(section, 2) == 0
    own = pl.ds(pl.multiple_of(me * rows, rows), rows)
    kv_in = (kf, vf, kb, vb)

    def remote(src, dst, send, recv, **where):
        return pltpu.make_async_remote_copy(
            src_ref=src, dst_ref=dst, send_sem=send, recv_sem=recv,
            device_id=where, device_id_type=pl.DeviceIdType.MESH,
        )

    def cols(c, size):
        return pl.ds(pl.multiple_of(c * size, size), size)

    def rows_of(j):
        return pl.ds(pl.multiple_of(j * rows, rows), rows)

    def docs_copy():
        return remote(docs.at[0], docs_r, docs_sem.at[0], docs_sem.at[1], pipe=before)

    def g_copy(c):
        at = cols(c, qw)
        return remote(cot.at[0, :, at], g_v.at[:, at], g_send.at[c], g_recv.at[c], pipe=before)

    def kv_copy(a, c, target, source):
        at = cols(c, hd)
        return remote(
            kv_in[a].at[0, :, at], kv.at[a, rows_of(source), at],
            kv_send.at[a, target, c], kv_recv.at[a, source, c], ctx=target,
        )

    def part_copy(a, c, target, source):
        at = cols(c, hd)
        return remote(
            dkv.at[a, rows_of(target), at], part.at[a, rows_of(source), at],
            part_send.at[a, target, c], part_recv.at[a, source, c], ctx=target,
        )

    def att_copy(c):
        at = cols(c, qw)
        return remote(
            att_s.at[:, at], att_o.at[0, :, at], wide_send.at[0, c], wide_recv.at[0, c], pipe=after
        )

    def dq_copy(c):
        at = cols(c, qw)
        return remote(
            dq_s.at[:, at], dq_o.at[0, :, at], wide_send.at[1, c], wide_recv.at[1, c], pipe=before
        )

    def dkv_copy(a, c):
        at = cols(c, hd)
        return remote(
            dkv_s.at[a, :, at], (dk_o, dv_o)[a].at[0, :, at],
            dkv_send.at[a, c], dkv_recv.at[a, c], pipe=before,
        )

    locals_ = [
        pltpu.make_async_copy(docs.at[0], docs_v, local_sem.at[0]),
        pltpu.make_async_copy(qf.at[0], qf_v, local_sem.at[1]),
        pltpu.make_async_copy(qb.at[0], qb_v, local_sem.at[2]),
    ] + [
        pltpu.make_async_copy(kv_in[a].at[0], kv.at[a, own], local_sem.at[3 + a]) for a in range(4)
    ]
    barrier = pltpu.get_barrier_semaphore()
    for where in (after, before):
        pl.semaphore_signal(
            barrier, inc=1, device_id={"pipe": where}, device_id_type=pl.DeviceIdType.MESH
        )
    for d in range(1, shards):
        pl.semaphore_signal(
            barrier, inc=1, device_id={"ctx": lax.rem(me + d, shards)},
            device_id_type=pl.DeviceIdType.MESH,
        )
    for copy in locals_:
        copy.start()
    for j in range(1, shards):

        @pl.when(j > me)
        def _():
            kv[:, j * rows : (j + 1) * rows, :] = jnp.zeros((4, rows, narrow), BF16)

    pl.semaphore_wait(barrier, shards + 1)
    docs_copy().start()

    def send_inputs(t, _):
        c = lax.rem(t, KVH)
        backward = (t < KVH) == even

        @pl.when(t < KVH)
        def _():
            g_copy(c).start()

        for j in range(1, shards):

            @pl.when(jnp.logical_and(j > me, backward))
            def _():
                kv_copy(2, c, j, me).start()
                kv_copy(3, c, j, me).start()

            @pl.when(jnp.logical_and(j > me, jnp.logical_not(backward)))
            def _():
                kv_copy(0, c, j, me).start()
                kv_copy(1, c, j, me).start()

        return 0

    lax.fori_loop(0, 2 * KVH, send_inputs, 0)
    for copy in locals_:
        copy.wait()
    docs_copy().wait_recv()

    for which, table in ((0, docs_r), (1, docs_v)):
        query_doc = table[which : which + 1, own].astype(F32)
        query_place = me * rows + lax.broadcasted_iota(jnp.int32, (rows, rows), 1)
        for j in range(shards):
            row = table[which : which + 1, j * rows : (j + 1) * rows].astype(F32)
            key_doc = jnp.transpose(jnp.broadcast_to(row, (rows, rows)))
            key_place = j * rows + lax.broadcasted_iota(jnp.int32, (rows, rows), 0)
            seen = jnp.logical_and(key_doc == query_doc, key_place <= query_place)
            bias[which, j * rows : (j + 1) * rows, :] = jnp.where(seen, F32(0), F32(-1e30))

    def stacked(ref, c):
        whole = ref[:, cols(c, qw)]
        return jnp.concatenate([whole[:, g * hd : (g + 1) * hd] for g in range(group)], axis=0)

    def probabilities(raw, which):
        masked = raw + bias[which]
        top = jnp.max(masked, axis=0, keepdims=True)
        power = jnp.exp2((masked - top) * F32(scale * math.log2(math.e)))
        return power * (F32(1) / jnp.sum(power, axis=0, keepdims=True))

    def forward(c):
        for j in range(shards - 1):

            @pl.when(j < me)
            def _():
                kv_copy(0, c, me, j).wait_recv()
                kv_copy(1, c, me, j).wait_recv()

        at = cols(c, hd)
        keys, values = kv[0, :, at], kv[1, :, at]
        raw = matmul(keys, stacked(qf_v, c), 1, 1)
        weights = jnp.concatenate(
            [
                probabilities(raw[:, g * rows : (g + 1) * rows], 0).astype(BF16)
                for g in range(group)
            ],
            axis=1,
        )
        mixed = matmul(weights, values, 0, 0)
        att_s[:, cols(c, qw)] = jnp.concatenate(
            [mixed[g * rows : (g + 1) * rows] for g in range(group)], axis=1
        ).astype(BF16)
        att_copy(c).start()

    def backward(c):
        for j in range(shards - 1):

            @pl.when(j < me)
            def _():
                kv_copy(2, c, me, j).wait_recv()
                kv_copy(3, c, me, j).wait_recv()

        g_copy(c).wait_recv()
        at = cols(c, hd)
        keys, values = kv[2, :, at], kv[3, :, at]
        queries, cotan = stacked(qb_v, c), stacked(g_v, c)
        raw = matmul(keys, queries, 1, 1)
        prob_grad = matmul(values, cotan, 1, 1)
        weights, score_grad = [], []
        for g in range(group):
            probs = probabilities(raw[:, g * rows : (g + 1) * rows], 1)
            grad = prob_grad[:, g * rows : (g + 1) * rows]
            delta = jnp.sum(probs * grad, axis=0, keepdims=True)
            weights.append(probs.astype(BF16))
            score_grad.append((probs * (grad - delta) * F32(scale)).astype(BF16))
        weights = jnp.concatenate(weights, axis=1)
        score_grad = jnp.concatenate(score_grad, axis=1)
        dq = matmul(score_grad, keys, 0, 0)
        dq_s[:, cols(c, qw)] = jnp.concatenate(
            [dq[g * rows : (g + 1) * rows] for g in range(group)], axis=1
        ).astype(BF16)
        dq_copy(c).start()
        dkv[0, :, at] = matmul(score_grad, queries, 1, 0)
        dkv[1, :, at] = matmul(weights, cotan, 1, 0)
        for j in range(shards - 1):

            @pl.when(j < me)
            def _():
                part_copy(0, c, j, me).start()
                part_copy(1, c, j, me).start()

    def step(t, _):
        c = lax.rem(t, KVH)
        is_backward = (t < KVH) == even
        pl.when(is_backward)(lambda: backward(c))
        pl.when(jnp.logical_not(is_backward))(lambda: forward(c))
        return 0

    lax.fori_loop(0, 2 * KVH, step, 0)

    def combine(c, _):
        at = cols(c, hd)
        for a in range(2):
            for j in range(1, shards):

                @pl.when(j > me)
                def _():
                    part_copy(a, c, me, j).wait_recv()
                    dkv[a, own, at] += part[a, j * rows : (j + 1) * rows, at]

            dkv_s[a, :, at] = dkv[a, own, at].astype(BF16)
            dkv_copy(a, c).start()
        return 0

    lax.fori_loop(0, KVH, combine, 0)

    docs_copy().wait_send()

    def finish(c, _):
        g_copy(c).wait_send()
        for a in range(4):
            for j in range(1, shards):
                pl.when(j > me)(lambda: kv_copy(a, c, j, me).wait_send())
        for a in range(2):
            for j in range(shards - 1):
                pl.when(j < me)(lambda: part_copy(a, c, j, me).wait_send())
        for copy in (att_copy(c), dq_copy(c), dkv_copy(0, c), dkv_copy(1, c)):
            copy.wait_send()
            copy.wait_recv()
        return 0

    lax.fori_loop(0, KVH, finish, 0)


def on_device(*args):
    query, key, documents = args[0], args[1], args[7]
    sections, shards = lax.axis_size("pipe"), lax.axis_size("ctx")
    rows, width = query.shape[1:]
    narrow = key.shape[2]
    seq = rows * shards
    dma = pltpu.SemaphoreType.DMA
    anywhere = pl.BlockSpec(memory_space=pl.ANY)
    return pl.pallas_call(
        functools.partial(kernel, sections, shards),
        name="relay_attention",
        out_shape=[
            jax.ShapeDtypeStruct(query.shape, BF16),
            jax.ShapeDtypeStruct(query.shape, BF16),
            jax.ShapeDtypeStruct(key.shape, BF16),
            jax.ShapeDtypeStruct(key.shape, BF16),
        ],
        in_specs=[anywhere] * 8,
        out_specs=[anywhere] * 4,
        scratch_shapes=[
            pltpu.VMEM((rows, width), BF16),
            pltpu.VMEM((rows, width), BF16),
            pltpu.VMEM((rows, width), BF16),
            pltpu.VMEM((4, seq, narrow), BF16),
            pltpu.VMEM((rows, width), BF16),
            pltpu.VMEM((rows, width), BF16),
            pltpu.VMEM((2, rows, narrow), BF16),
            pltpu.VMEM((2, seq, narrow), F32),
            pltpu.VMEM((2, seq, narrow), F32),
            pltpu.VMEM(documents.shape[1:], jnp.int32),
            pltpu.VMEM(documents.shape[1:], jnp.int32),
            pltpu.VMEM((2, seq, rows), F32),
            dma((7,)),
            dma((2,)),
            dma((4, shards, KVH)),
            dma((4, shards, KVH)),
            dma((KVH,)),
            dma((KVH,)),
            dma((2, shards, KVH)),
            dma((2, shards, KVH)),
            dma((2, KVH)),
            dma((2, KVH)),
            dma((2, KVH)),
            dma((2, KVH)),
        ],
        compiler_params=pltpu.CompilerParams(
            collective_id=0, has_side_effects=True, vmem_limit_bytes=56 * 2**20
        ),
    )(*args)


def solution(mesh):
    split = P("pipe", "ctx", None)
    return jax.shard_map(
        on_device,
        mesh=mesh,
        in_specs=(split,) * 7 + (P("pipe", None, None),),
        out_specs=(split,) * 4,
        check_vma=False,
    )
```

time: 233 us -> 54 us (0.23)
  the two profiles are of different devices: /device:TPU:0 before, /device:TPU:28 now
where the time goes in v1:
time: 54 us; the launch traced here: 53.8 us
  Pallas kernels  47.9 us (89%)
  local copies, waits for them, and re-layouts  5.22 us (10%)
  between operations  0.65 us (1%)
    pallas_call x1, Pallas kernels, on_device(): pl.pallas_call(functools.partial(kernel, sections, shards), name='relay_a...  47.9 us
    unnamed x10, local copies, waits for them, and re-layouts  5.22 us

profile of v1, /device:TPU:28, one launch (start us, length us, event | category | flops | bytes accessed | tf_op | source)
XLA Modules:
  0.0 53.8 jit_solution(3213463970840886192)
XLA Ops:
  0.6 47.9 %relay_attention.1 = (bf16[1,128,4096]{2,1,0:T(8,128)(2,1)}, bf16[1,128,4096]{2,1,0:T(8,128)(2,1)}, bf16[1,128,1024]{2,1,0:T(8,128)(2,1)}, bf16[1,128,1024]{2,1,0:T(8,128)(2,1)}) custom-call(bf16[1,128,4096]{2,1,0:T(8,128)(2,1)} %qf.1, bf16[1,128,1024]{2,1,0:T(8,128)(2,1)} %kf.1, bf16[1,128,1024]{2,1,0:T(8,128)(2,1)} %vf.1, bf16[1,128,4096]{2,1,0:T(8,128)(2,1)} %qb.1, ...), custom_call_target="tpu_custom_call" | custom-call | tf_op jit(solution)/shard_map/relay_attention/pallas_call | solution.py:278
  48.6 0.0 copy-start
  48.6 2.4 %copy.16 = bf16[1,128,4096]{2,1,0:T(8,128)(2,1)} copy(bf16[1,128,4096]{2,1,0:T(8,128)(2,1)} %get-tuple-element.8) | data formatting | bytes 2097152
  50.9 0.0 copy-done
  51.0 0.0 copy-start.2
  51.0 1.0 %copy.17 = bf16[1,128,4096]{2,1,0:T(8,128)(2,1)} copy(bf16[1,128,4096]{2,1,0:T(8,128)(2,1)S(1)} %copy-done) | data formatting | bytes 2097152
  51.9 0.1 copy-done.2
  52.0 0.0 copy-start.1
  52.0 0.7 %copy.18 = bf16[1,128,1024]{2,1,0:T(8,128)(2,1)} copy(bf16[1,128,1024]{2,1,0:T(8,128)(2,1)S(1)} %copy-done.2) | data formatting | bytes 524288
  52.7 0.3 copy-done.1
  53.1 0.7 %copy.19 = bf16[1,128,1024]{2,1,0:T(8,128)(2,1)} copy(bf16[1,128,1024]{2,1,0:T(8,128)(2,1)S(1)} %copy-done.1) | data formatting | bytes 524288
Async XLA Ops:
  48.6 2.4 %copy-start = (bf16[1,128,4096]{2,1,0:T(8,128)(2,1)S(1)}, bf16[1,128,4096]{2,1,0:T(8,128)(2,1)}, u32[]{:S(2)}) copy-start(bf16[1,128,4096]{2,1,0:T(8,128)(2,1)} %get-tuple-element.9) | copy-start | bytes 3145732
  51.0 1.1 %copy-start.2 = (bf16[1,128,1024]{2,1,0:T(8,128)(2,1)S(1)}, bf16[1,128,1024]{2,1,0:T(8,128)(2,1)}, u32[]{:S(2)}) copy-start(bf16[1,128,1024]{2,1,0:T(8,128)(2,1)} %get-tuple-element.10) | copy-start | bytes 786436
  52.0 1.0 %copy-start.1 = (bf16[1,128,1024]{2,1,0:T(8,128)(2,1)S(1)}, bf16[1,128,1024]{2,1,0:T(8,128)(2,1)}, u32[]{:S(2)}) copy-start(bf16[1,128,1024]{2,1,0:T(8,128)(2,1)} %get-tuple-element.11) | copy-start | bytes 786436

commit v2 on v1

--- a/solution.py
+++ b/solution.py
@@ -267,6 +267,28 @@
     lax.fori_loop(0, KVH, finish, 0)
 
 
+def store_kernel(*refs):
+    half = len(refs) // 2
+    sems = refs[-1]
+    copies = [pltpu.make_async_copy(refs[i], refs[half + i], sems.at[i]) for i in range(half)]
+    for copy in copies:
+        copy.start()
+    for copy in copies:
+        copy.wait()
+
+
+def stored(arrays):
+    anywhere = pl.BlockSpec(memory_space=pl.ANY)
+    return pl.pallas_call(
+        store_kernel,
+        name="store_outputs",
+        out_shape=[pltpu.HBM(array.shape, array.dtype) for array in arrays],
+        in_specs=[pl.BlockSpec(memory_space=pltpu.VMEM)] * len(arrays),
+        out_specs=[anywhere] * len(arrays),
+        scratch_shapes=[pltpu.SemaphoreType.DMA((len(arrays),))],
+    )(*[pltpu.with_memory_space_constraint(array, pltpu.VMEM) for array in arrays])
+
+
 def on_device(*args):
     query, key, documents = args[0], args[1], args[7]
     sections, shards = lax.axis_size("pipe"), lax.axis_size("ctx")
@@ -275,17 +297,17 @@
     seq = rows * shards
     dma = pltpu.SemaphoreType.DMA
     anywhere = pl.BlockSpec(memory_space=pl.ANY)
-    return pl.pallas_call(
+    return stored(pl.pallas_call(
         functools.partial(kernel, sections, shards),
         name="relay_attention",
         out_shape=[
-            jax.ShapeDtypeStruct(query.shape, BF16),
-            jax.ShapeDtypeStruct(query.shape, BF16),
-            jax.ShapeDtypeStruct(key.shape, BF16),
-            jax.ShapeDtypeStruct(key.shape, BF16),
+            pltpu.VMEM(query.shape, BF16),
+            pltpu.VMEM(query.shape, BF16),
+            pltpu.VMEM(key.shape, BF16),
+            pltpu.VMEM(key.shape, BF16),
         ],
         in_specs=[anywhere] * 8,
-        out_specs=[anywhere] * 4,
+        out_specs=[pl.BlockSpec(memory_space=pltpu.VMEM)] * 4,
         scratch_shapes=[
             pltpu.VMEM((rows, width), BF16),
             pltpu.VMEM((rows, width), BF16),
@@ -315,7 +337,7 @@
         compiler_params=pltpu.CompilerParams(
             collective_id=0, has_side_effects=True, vmem_limit_bytes=56 * 2**20
         ),
-    )(*args)
+    )(*args))
 
 
 def solution(mesh):

time: 54 us -> 50.1 us (0.928)
  local copies, waits for them, and re-layouts: 5.22 us -> 0 us
  Pallas kernels: 47.9 us -> 49.3 us
    unnamed x10 -> x0, local copies, waits for them, and re-layouts: 5.22 us -> none
    pallas_call x0 -> x1, Pallas kernels: none -> 1.52 us  [stored(): pl.pallas_call(store_kernel, name='store_outputs', out_shape=[pltpu.HBM(a...]
where the time goes in v2:
time: 50.1 us; the launch traced here: 50 us
  Pallas kernels  49.3 us (98%)
  between operations  0.64 us (1%)
    pallas_call x1, Pallas kernels, on_device(): pl.pallas_call(functools.partial(kernel, sections, shards), name='relay_a...  47.8 us
    pallas_call x1, Pallas kernels, stored(): pl.pallas_call(store_kernel, name='store_outputs', out_shape=[pltpu.HBM(a...  1.52 us

profile of v2, /device:TPU:28, one launch (start us, length us, event | category | flops | bytes accessed | tf_op | source)
XLA Modules:
  0.0 50.0 jit_solution(1877088892125255157)
XLA Ops:
  0.6 47.8 %relay_attention.1 = (bf16[1,128,4096]{2,1,0:T(8,128)(2,1)S(1)}, bf16[1,128,4096]{2,1,0:T(8,128)(2,1)S(1)}, bf16[1,128,1024]{2,1,0:T(8,128)(2,1)S(1)}, bf16[1,128,1024]{2,1,0:T(8,128)(2,1)S(1)}) custom-call(bf16[1,128,4096]{2,1,0:T(8,128)(2,1)} %qf.1, bf16[1,128,1024]{2,1,0:T(8,128)(2,1)} %kf.1, bf16[1,128,1024]{2,1,0:T(8,128)(2,1)} %vf.1, ...), custom_call_target="tpu_custom_call" | custom-call | tf_op jit(solution)/shard_map/relay_attention/pallas_call | solution.py:300
  48.5 1.5 %store_outputs.1 = (bf16[1,128,4096]{2,1,0:T(8,128)(2,1)}, bf16[1,128,4096]{2,1,0:T(8,128)(2,1)}, bf16[1,128,1024]{2,1,0:T(8,128)(2,1)}, bf16[1,128,1024]{2,1,0:T(8,128)(2,1)}) custom-call(bf16[1,128,4096]{2,1,0:T(8,128)(2,1)S(1)} %get-tuple-element.8.refs_0_, bf16[1,128,4096]{2,1,0:T(8,128)(2,1)S(1)} %get-tuple-element.9.refs_1_, ...), custom_call_target="tpu_custom_call" | custom-call | tf_op jit(solution)/shard_map/store_outputs/pallas_call | solution.py:282

commit v3 on v2

--- a/solution.py
+++ b/solution.py
@@ -9,6 +9,7 @@
 from jax.sharding import PartitionSpec as P
 
 KVH = 8
+PIECES = 4
 F32 = jnp.float32
 BF16 = jnp.bfloat16
 
@@ -224,16 +225,7 @@
                 part_copy(0, c, j, me).start()
                 part_copy(1, c, j, me).start()
 
-    def step(t, _):
-        c = lax.rem(t, KVH)
-        is_backward = (t < KVH) == even
-        pl.when(is_backward)(lambda: backward(c))
-        pl.when(jnp.logical_not(is_backward))(lambda: forward(c))
-        return 0
-
-    lax.fori_loop(0, 2 * KVH, step, 0)
-
-    def combine(c, _):
+    def combine(c):
         at = cols(c, hd)
         for a in range(2):
             for j in range(1, shards):
@@ -245,9 +237,20 @@
 
             dkv_s[a, :, at] = dkv[a, own, at].astype(BF16)
             dkv_copy(a, c).start()
+
+    def step(t, _):
+        c = lax.rem(t, KVH)
+        early, odd = t < KVH, jnp.logical_not(even)
+
+        @pl.when(jnp.logical_and(t >= KVH, jnp.logical_or(even, t >= 2 * KVH)))
+        def _():
+            combine(c)
+
+        pl.when(jnp.logical_and(t < 2 * KVH, early == even))(lambda: backward(c))
+        pl.when(jnp.logical_and(t < 2 * KVH, early == odd))(lambda: forward(c))
         return 0
 
-    lax.fori_loop(0, KVH, combine, 0)
+    lax.fori_loop(0, jnp.where(even, 2 * KVH, 3 * KVH), step, 0)
 
     docs_copy().wait_send()
 
@@ -270,7 +273,14 @@
 def store_kernel(*refs):
     half = len(refs) // 2
     sems = refs[-1]
-    copies = [pltpu.make_async_copy(refs[i], refs[half + i], sems.at[i]) for i in range(half)]
+    copies = []
+    for i in range(half):
+        piece = refs[i].shape[1] // PIECES
+        for k in range(PIECES):
+            at = (0, slice(k * piece, (k + 1) * piece))
+            copies.append(
+                pltpu.make_async_copy(refs[i].at[at], refs[half + i].at[at], sems.at[i, k])
+            )
     for copy in copies:
         copy.start()
     for copy in copies:
@@ -285,7 +295,7 @@
         out_shape=[pltpu.HBM(array.shape, array.dtype) for array in arrays],
         in_specs=[pl.BlockSpec(memory_space=pltpu.VMEM)] * len(arrays),
         out_specs=[anywhere] * len(arrays),
-        scratch_shapes=[pltpu.SemaphoreType.DMA((len(arrays),))],
+        scratch_shapes=[pltpu.SemaphoreType.DMA((len(arrays), PIECES))],
     )(*[pltpu.with_memory_space_constraint(array, pltpu.VMEM) for array in arrays])
 
 

time: 50.1 us -> 50.2 us (level)
  no operation moved by 1% of the time
where the time goes in v3:
time: 50.2 us; the launch traced here: 50.1 us
  Pallas kernels  49.4 us (98%)
  between operations  0.64 us (1%)
    pallas_call x1, Pallas kernels, on_device(): pl.pallas_call(functools.partial(kernel, sections, shards), name='relay_a...  47.8 us
    pallas_call x1, Pallas kernels, stored(): pl.pallas_call(store_kernel, name='store_outputs', out_shape=[pltpu.HBM(a...  1.61 us

profile of v3, /device:TPU:28, one launch (start us, length us, event | category | flops | bytes accessed | tf_op | source)
XLA Modules:
  0.0 50.1 jit_solution(11654260173910314112)
XLA Ops:
  0.6 47.8 %relay_attention.1 = (bf16[1,128,4096]{2,1,0:T(8,128)(2,1)S(1)}, bf16[1,128,4096]{2,1,0:T(8,128)(2,1)S(1)}, bf16[1,128,1024]{2,1,0:T(8,128)(2,1)S(1)}, bf16[1,128,1024]{2,1,0:T(8,128)(2,1)S(1)}) custom-call(bf16[1,128,4096]{2,1,0:T(8,128)(2,1)} %qf.1, bf16[1,128,1024]{2,1,0:T(8,128)(2,1)} %kf.1, bf16[1,128,1024]{2,1,0:T(8,128)(2,1)} %vf.1, ...), custom_call_target="tpu_custom_call" | custom-call | tf_op jit(solution)/shard_map/relay_attention/pallas_call | solution.py:310
  48.5 1.6 %store_outputs.1 = (bf16[1,128,4096]{2,1,0:T(8,128)(2,1)}, bf16[1,128,4096]{2,1,0:T(8,128)(2,1)}, bf16[1,128,1024]{2,1,0:T(8,128)(2,1)}, bf16[1,128,1024]{2,1,0:T(8,128)(2,1)}) custom-call(bf16[1,128,4096]{2,1,0:T(8,128)(2,1)S(1)} %get-tuple-element.8.refs_0_, bf16[1,128,4096]{2,1,0:T(8,128)(2,1)S(1)} %get-tuple-element.9.refs_1_, ...), custom_call_target="tpu_custom_call" | custom-call | tf_op jit(solution)/shard_map/store_outputs/pallas_call | solution.py:292

commit v4 on v3

--- a/solution.py
+++ b/solution.py
@@ -9,7 +9,7 @@
 from jax.sharding import PartitionSpec as P
 
 KVH = 8
-PIECES = 4
+SPAN = 4
 F32 = jnp.float32
 BF16 = jnp.bfloat16
 
@@ -83,7 +83,7 @@
         )
 
     def dkv_copy(a, c):
-        at = cols(c, hd)
+        at = cols(c, SPAN * hd)
         return remote(
             dkv_s.at[a, :, at], (dk_o, dv_o)[a].at[0, :, at],
             dkv_send.at[a, c], dkv_recv.at[a, c], pipe=before,
@@ -236,7 +236,11 @@
                     dkv[a, own, at] += part[a, j * rows : (j + 1) * rows, at]
 
             dkv_s[a, :, at] = dkv[a, own, at].astype(BF16)
-            dkv_copy(a, c).start()
+
+        @pl.when(lax.rem(c, SPAN) == SPAN - 1)
+        def _():
+            dkv_copy(0, lax.div(c, SPAN)).start()
+            dkv_copy(1, lax.div(c, SPAN)).start()
 
     def step(t, _):
         c = lax.rem(t, KVH)
@@ -262,25 +266,22 @@
         for a in range(2):
             for j in range(shards - 1):
                 pl.when(j < me)(lambda: part_copy(a, c, j, me).wait_send())
-        for copy in (att_copy(c), dq_copy(c), dkv_copy(0, c), dkv_copy(1, c)):
+        for copy in (att_copy(c), dq_copy(c)):
             copy.wait_send()
             copy.wait_recv()
         return 0
 
     lax.fori_loop(0, KVH, finish, 0)
+    for a in range(2):
+        for c in range(KVH // SPAN):
+            dkv_copy(a, c).wait_send()
+            dkv_copy(a, c).wait_recv()
 
 
 def store_kernel(*refs):
     half = len(refs) // 2
     sems = refs[-1]
-    copies = []
-    for i in range(half):
-        piece = refs[i].shape[1] // PIECES
-        for k in range(PIECES):
-            at = (0, slice(k * piece, (k + 1) * piece))
-            copies.append(
-                pltpu.make_async_copy(refs[i].at[at], refs[half + i].at[at], sems.at[i, k])
-            )
+    copies = [pltpu.make_async_copy(refs[i], refs[half + i], sems.at[i]) for i in range(half)]
     for copy in copies:
         copy.start()
     for copy in copies:
@@ -295,7 +296,7 @@
         out_shape=[pltpu.HBM(array.shape, array.dtype) for array in arrays],
         in_specs=[pl.BlockSpec(memory_space=pltpu.VMEM)] * len(arrays),
         out_specs=[anywhere] * len(arrays),
-        scratch_shapes=[pltpu.SemaphoreType.DMA((len(arrays), PIECES))],
+        scratch_shapes=[pltpu.SemaphoreType.DMA((len(arrays),))],
     )(*[pltpu.with_memory_space_constraint(array, pltpu.VMEM) for array in arrays])
 
 
@@ -341,8 +342,8 @@
             dma((2, shards, KVH)),
             dma((2, KVH)),
             dma((2, KVH)),
-            dma((2, KVH)),
-            dma((2, KVH)),
+            dma((2, KVH // SPAN)),
+            dma((2, KVH // SPAN)),
         ],
         compiler_params=pltpu.CompilerParams(
             collective_id=0, has_side_effects=True, vmem_limit_bytes=56 * 2**20

time: 50.2 us -> 49.9 us (level)
  no operation moved by 1% of the time
where the time goes in v4:
time: 49.9 us; the launch traced here: 49.8 us
  Pallas kernels  49.1 us (98%)
  between operations  0.64 us (1%)
    pallas_call x1, Pallas kernels, on_device(): pl.pallas_call(functools.partial(kernel, sections, shards), name='relay_a...  47.6 us
    pallas_call x1, Pallas kernels, stored(): pl.pallas_call(store_kernel, name='store_outputs', out_shape=[pltpu.HBM(a...  1.52 us

profile of v4, /device:TPU:28, one launch (start us, length us, event | category | flops | bytes accessed | tf_op | source)
XLA Modules:
  0.0 49.8 jit_solution(8693435564225086916)
XLA Ops:
  0.6 47.6 %relay_attention.1 = (bf16[1,128,4096]{2,1,0:T(8,128)(2,1)S(1)}, bf16[1,128,4096]{2,1,0:T(8,128)(2,1)S(1)}, bf16[1,128,1024]{2,1,0:T(8,128)(2,1)S(1)}, bf16[1,128,1024]{2,1,0:T(8,128)(2,1)S(1)}) custom-call(bf16[1,128,4096]{2,1,0:T(8,128)(2,1)} %qf.1, bf16[1,128,1024]{2,1,0:T(8,128)(2,1)} %kf.1, bf16[1,128,1024]{2,1,0:T(8,128)(2,1)} %vf.1, ...), custom_call_target="tpu_custom_call" | custom-call | tf_op jit(solution)/shard_map/relay_attention/pallas_call | solution.py:311
  48.2 1.5 %store_outputs.1 = (bf16[1,128,4096]{2,1,0:T(8,128)(2,1)}, bf16[1,128,4096]{2,1,0:T(8,128)(2,1)}, bf16[1,128,1024]{2,1,0:T(8,128)(2,1)}, bf16[1,128,1024]{2,1,0:T(8,128)(2,1)}) custom-call(bf16[1,128,4096]{2,1,0:T(8,128)(2,1)S(1)} %get-tuple-element.8.refs_0_, bf16[1,128,4096]{2,1,0:T(8,128)(2,1)S(1)} %get-tuple-element.9.refs_1_, ...), custom_call_target="tpu_custom_call" | custom-call | tf_op jit(solution)/shard_map/store_outputs/pallas_call | solution.py:293

commit v5 on v4

--- a/solution.py
+++ b/solution.py
@@ -115,15 +115,14 @@
             kv[:, j * rows : (j + 1) * rows, :] = jnp.zeros((4, rows, narrow), BF16)
 
     pl.semaphore_wait(barrier, shards + 1)
-    docs_copy().start()
+    for c in range(KVH):
+        g_copy(c).start()
+        if c == 0:
+            docs_copy().start()
 
     def send_inputs(t, _):
         c = lax.rem(t, KVH)
         backward = (t < KVH) == even
-
-        @pl.when(t < KVH)
-        def _():
-            g_copy(c).start()
 
         for j in range(1, shards):
 

time: 49.9 us -> 49.9 us (level)
  no operation moved by 1% of the time
where the time goes in v5:
time: 49.9 us; the launch traced here: 49.8 us
  Pallas kernels  49.1 us (98%)
  between operations  0.64 us (1%)
    pallas_call x1, Pallas kernels, on_device(): pl.pallas_call(functools.partial(kernel, sections, shards), name='relay_a...  47.6 us
    pallas_call x1, Pallas kernels, stored(): pl.pallas_call(store_kernel, name='store_outputs', out_shape=[pltpu.HBM(a...  1.52 us

profile of v5, /device:TPU:28, one launch (start us, length us, event | category | flops | bytes accessed | tf_op | source)
XLA Modules:
  0.0 49.8 jit_solution(3522877872795224662)
XLA Ops:
  0.6 47.6 %relay_attention.1 = (bf16[1,128,4096]{2,1,0:T(8,128)(2,1)S(1)}, bf16[1,128,4096]{2,1,0:T(8,128)(2,1)S(1)}, bf16[1,128,1024]{2,1,0:T(8,128)(2,1)S(1)}, bf16[1,128,1024]{2,1,0:T(8,128)(2,1)S(1)}) custom-call(bf16[1,128,4096]{2,1,0:T(8,128)(2,1)} %qf.1, bf16[1,128,1024]{2,1,0:T(8,128)(2,1)} %kf.1, bf16[1,128,1024]{2,1,0:T(8,128)(2,1)} %vf.1, ...), custom_call_target="tpu_custom_call" | custom-call | tf_op jit(solution)/shard_map/relay_attention/pallas_call | solution.py:310
  48.3 1.5 %store_outputs.1 = (bf16[1,128,4096]{2,1,0:T(8,128)(2,1)}, bf16[1,128,4096]{2,1,0:T(8,128)(2,1)}, bf16[1,128,1024]{2,1,0:T(8,128)(2,1)}, bf16[1,128,1024]{2,1,0:T(8,128)(2,1)}) custom-call(bf16[1,128,4096]{2,1,0:T(8,128)(2,1)S(1)} %get-tuple-element.8.refs_0_, bf16[1,128,4096]{2,1,0:T(8,128)(2,1)S(1)} %get-tuple-element.9.refs_1_, ...), custom_call_target="tpu_custom_call" | custom-call | tf_op jit(solution)/shard_map/store_outputs/pallas_call | solution.py:292
